TPU v7x, 32 devices: a whole 2x2x4 slice. The times are simulated.
32 devices in a mesh: dp: 4 (over y, core), row: 2 (over x), col: 4 (over z).
Axes of the slice: x: 2, y: 2, z: 4, core: 2. Of those that a mesh axis runs over, the one named last changes fastest.
Arguments:
- hidden_in: bfloat16 [5120, 2048], P(('dp', 'col'), 'row'), may hold values from -6 to 6
- seq_lengths: int32 [4], P('dp'), may hold values from 512 to 1280, as said below
- gain_attn: bfloat16 [2048], P('row'), may hold values from 0.5 to 1.5
- w_query: bfloat16 [2048, 2048], P('row', 'col'), may hold values from -0.125 to 0.125
- w_key: bfloat16 [2048, 2048], P('row', 'col'), may hold values from -0.125 to 0.125
- w_value: bfloat16 [2048, 2048], P('row', 'col'), may hold values from -0.125 to 0.125
- w_outgate: bfloat16 [2048, 2048], P('row', 'col'), may hold values from -0.125 to 0.125
- rank_down: bfloat16 [2048, 16], P('row'), may hold values from -0.125 to 0.125
- rank_up: bfloat16 [16, 2048], P(None, 'col'), may hold values from -1.5 to 1.5
- decay_bias: float32 [2048], P('col'), may hold values from -1 to 7
- gain_head: bfloat16 [512], P('row'), may hold values from 0.5 to 1.5
- w_output: bfloat16 [2048, 2048], P('col', 'row'), may hold values from -0.1875 to 0.1875
- gain_ffn: bfloat16 [2048], P('row'), may hold values from 0.5 to 1.5
- w_gate: bfloat16 [2048, 5632], P('row', 'col'), may hold values from -0.125 to 0.125
- w_up: bfloat16 [2048, 5632], P('row', 'col'), may hold values from -0.125 to 0.125
- w_down: bfloat16 [5632, 2048], P('col', 'row'), may hold values from -0.109375 to 0.109375
- cotangent: bfloat16 [5120, 2048], P(('dp', 'col'), 'row'), may hold values from -6 to 6
Outputs:
- block_out: bfloat16 [5120, 2048], P(('dp', 'col'), 'row')
- grad_input: float32 [5120, 2048], P(('dp', 'col'), 'row')
- grad_gain_attn: float32 [2048], P('row')
- grad_w_query: float32 [2048, 2048], P('row', 'col')
- grad_w_key: float32 [2048, 2048], P('row', 'col')
- grad_w_value: float32 [2048, 2048], P('row', 'col')
- grad_w_outgate: float32 [2048, 2048], P('row', 'col')
- grad_rank_down: float32 [2048, 16], P('row')
- grad_rank_up: float32 [16, 2048], P(None, 'col')
- grad_decay_bias: float32 [2048], P('col')
- grad_gain_head: float32 [512], P('row')
- grad_w_output: float32 [2048, 2048], P('col', 'row')
- grad_gain_ffn: float32 [2048], P('row')
- grad_w_gate: float32 [2048, 5632], P('row', 'col')
- grad_w_up: float32 [2048, 5632], P('row', 'col')
- grad_w_down: float32 [5632, 2048], P('col', 'row')
Inputs may be any that keep to these rules, and one draw needn't show every extreme that they name: `seq_lengths`: valid tokens of each slot of 1280 positions; every draw has one full slot and one slot of exactly 512 tokens.
All inputs are finite; a program needn't handle non-finite values.
Results may differ from a plain program's by a relative error of at most 0.025.
Values may be sent and summed in bfloat16 or wider, within the bound.
No kernel may reach another device: no remote copies, remote signals or barrier semaphores. Data moves between devices by JAX's collectives and lax.ppermute only.
A program may use at most 256 MiB of HBM per device.

v0:
```python
import math
import jax
import jax.numpy as jnp
from jax import lax
from jax.sharding import PartitionSpec as P

D = 2048
HEAD_K = 512
HEAD_V = 512
BLOCK = 64
SLOT = 1280
EPSILON = 1e-06
HIGHEST = lax.Precision.HIGHEST


def for_sending(x):

    def short(part):
        return part.astype(jnp.bfloat16) if part.dtype == jnp.float32 else part

    return jax.tree.map(short, x)


def product(left, right):
    return jnp.dot(left, right, preferred_element_type=jnp.float32)


def contract_rows(left, right):
    return lax.dot_general(
        left, right, (((0,), (0,)), ((), ())), preferred_element_type=jnp.float32
    )


def contract_cols(left, right):
    return lax.dot_general(
        left, right, (((1,), (1,)), ((), ())), preferred_element_type=jnp.float32
    )


def gla_sequence(queries, key_rows, value_rows, decays):
    block_count = queries.shape[0] // BLOCK
    key_extent = queries.shape[1]
    value_extent = value_rows.shape[1]
    query_blocks = queries.reshape(block_count, BLOCK, key_extent)
    key_blocks = key_rows.reshape(block_count, BLOCK, key_extent)
    value_blocks = value_rows.reshape(block_count, BLOCK, value_extent)
    decay_blocks = decays.reshape(block_count, BLOCK, key_extent)
    running = jnp.cumsum(decay_blocks, axis=1)
    ending = running[:, -1:, :]
    query_fade = query_blocks * jnp.exp(running)
    key_grow = key_blocks * jnp.exp(-running)
    key_final = key_blocks * jnp.exp(ending - running)
    causal = jnp.tril(jnp.ones((BLOCK, BLOCK), jnp.float32))
    scores = jnp.einsum("bik,bjk->bij", query_fade, key_grow, precision=HIGHEST) * causal
    within = jnp.einsum("bij,bjv->biv", scores, value_blocks, precision=HIGHEST)
    updates = jnp.einsum("bjk,bjv->bkv", key_final, value_blocks, precision=HIGHEST)
    fading = jnp.exp(ending[:, 0, :])

    def advance(carried, inputs_now):
        update_now, fade_now = inputs_now
        return (carried * fade_now[:, None] + update_now, carried)

    initial = jnp.zeros((key_extent, value_extent), jnp.float32)
    _, earlier = lax.scan(advance, initial, (updates, fading))
    across = jnp.einsum("bik,bkv->biv", query_fade, earlier, precision=HIGHEST)
    return (within + across).reshape(block_count * BLOCK, value_extent)


def row_total(partial_value):
    return lax.psum(partial_value, "row")


def norm_forward(values, gains, extent):
    summed = row_total(jnp.sum(values * values, axis=1))
    factor = lax.rsqrt(summed / extent + EPSILON)
    return (values * factor[:, None] * gains, factor)


def norm_backward(values, factor, gains, upstream, extent):
    weighted = upstream * gains
    inner_sum = row_total(jnp.sum(weighted * values, axis=1))
    grad_values = (
        factor[:, None] * weighted
        - values * (factor * factor * factor * inner_sum / extent)[:, None]
    )
    grad_gains = jnp.sum(upstream * values * factor[:, None], axis=0)
    return (grad_values, grad_gains)


def gather_tokens(tensor):
    return lax.all_gather(tensor, "col", axis=0, tiled=True)


def share_features(parts):
    return lax.psum_scatter(parts, "row", scatter_dimension=1, tiled=True)


def gather_features(parts):
    return jax.tree.map(
        lambda part, own: part.astype(own.dtype),
        lax.all_gather(for_sending(parts), "row", axis=1, tiled=True),
        parts,
    )


def reduce_tokens(builder, local_rows):
    return lax.psum_scatter(
        builder(jnp.int32(0), local_rows * lax.axis_size("col")),
        "col",
        scatter_dimension=0,
        tiled=True,
    )


def body(
    hidden_in,
    seq_lengths,
    gain_attn,
    w_query,
    w_key,
    w_value,
    w_outgate,
    rank_down,
    rank_up,
    decay_bias,
    gain_head,
    w_output,
    gain_ffn,
    w_gate,
    w_up,
    w_down,
    cotangent,
):
    local_rows = hidden_in.shape[0]
    col_index = lax.axis_index("col")
    row_index = lax.axis_index("row")
    group_rows = local_rows * lax.axis_size("col")
    key_share = HEAD_K // lax.axis_size("row")
    query_scale = 1.0 / math.sqrt(HEAD_K)
    places = jnp.arange(group_rows)
    owners = (places // SLOT)[:, None] == jnp.arange(seq_lengths.shape[0])[None, :]
    limits = jnp.sum(jnp.where(owners, seq_lengths[None, :], 0), axis=1)
    valid_group = (places % SLOT < limits).astype(jnp.float32)
    valid_here = lax.dynamic_slice_in_dim(valid_group, col_index * local_rows, local_rows)
    gain_attn_f = gain_attn.astype(jnp.float32)
    gain_head_f = gain_head.astype(jnp.float32)
    gain_ffn_f = gain_ffn.astype(jnp.float32)
    residual_in = hidden_in.astype(jnp.float32)
    normed_one, factor_one = norm_forward(residual_in, gain_attn_f, D)
    normed_one_low = normed_one.astype(jnp.bfloat16)
    tokens_one = gather_tokens(normed_one_low)
    query_part, key_part, outgate_share = share_features(
        (product(tokens_one, w_query), product(tokens_one, w_key), product(tokens_one, w_outgate))
    )
    value_full, rank_full = lax.psum(
        (product(tokens_one, w_value), product(tokens_one, rank_down)), "row"
    )
    query_low = query_part.astype(jnp.bfloat16)
    key_low = key_part.astype(jnp.bfloat16)
    value_low = value_full.astype(jnp.bfloat16)
    rank_low = rank_full.astype(jnp.bfloat16)
    rank_cols = lax.dynamic_slice_in_dim(rank_up, row_index * key_share, key_share, 1)
    bias_cols = lax.dynamic_slice_in_dim(decay_bias, row_index * key_share, key_share, 0)
    decay_logits = product(rank_low, rank_cols) + bias_cols
    decays = jax.nn.log_sigmoid(decay_logits) / 16.0

    def reshape_slots(tensor):
        return tensor.reshape(seq_lengths.shape[0], SLOT, tensor.shape[1])

    def attend(queries, key_rows, value_rows, decay_rows):
        mixed_slots = jax.vmap(gla_sequence)(
            reshape_slots(queries),
            reshape_slots(key_rows),
            reshape_slots(value_rows),
            reshape_slots(decay_rows),
        )
        return mixed_slots.reshape(group_rows, value_rows.shape[1])

    mixed_part, attend_back = jax.vjp(
        attend,
        query_low.astype(jnp.float32) * query_scale,
        key_low.astype(jnp.float32),
        value_low.astype(jnp.float32),
        decays,
    )
    mixed_share = share_features(mixed_part)
    normed_head, factor_head = norm_forward(mixed_share, gain_head_f, HEAD_V)
    outgate_sig = jax.nn.sigmoid(outgate_share)
    outgate_act = outgate_share * outgate_sig
    gated_share = (normed_head * outgate_act).astype(jnp.bfloat16)
    gated_all = gather_features(gated_share)

    def attn_rows(first_row, row_count):
        return product(gated_all, w_output)

    attn_out = reduce_tokens(attn_rows, local_rows)
    residual_mid = residual_in + attn_out
    normed_two, factor_two = norm_forward(residual_mid, gain_ffn_f, D)
    normed_two_low = normed_two.astype(jnp.bfloat16)
    tokens_two = gather_tokens(normed_two_low)
    gate_pre, up_pre = share_features((product(tokens_two, w_gate), product(tokens_two, w_up)))
    swish_sig = jax.nn.sigmoid(gate_pre)
    swish_out = gate_pre * swish_sig
    hidden_share = (swish_out * up_pre).astype(jnp.bfloat16)
    hidden_all = gather_features(hidden_share)

    def ffn_rows(first_row, row_count):
        return product(hidden_all, w_down)

    ffn_out = reduce_tokens(ffn_rows, local_rows)
    block_out = (valid_here[:, None] * (residual_mid + ffn_out)).astype(jnp.bfloat16)
    upstream = valid_here[:, None] * cotangent.astype(jnp.float32)
    ffn_grad_all = gather_tokens(upstream.astype(jnp.bfloat16))
    hidden_grad = share_features(contract_cols(ffn_grad_all, w_down))
    grad_down = contract_rows(hidden_all, ffn_grad_all)
    swish_slope = swish_sig * (1.0 + gate_pre * (1.0 - swish_sig))
    gate_grad = (hidden_grad * up_pre * swish_slope).astype(jnp.bfloat16)
    up_grad = (hidden_grad * swish_out).astype(jnp.bfloat16)
    gate_grad_all, up_grad_all = gather_features((gate_grad, up_grad))
    grad_gate = contract_rows(tokens_two, gate_grad_all)
    grad_up = contract_rows(tokens_two, up_grad_all)

    def norm_two_rows(first_row, row_count):
        return contract_cols(gate_grad_all, w_gate) + contract_cols(up_grad_all, w_up)

    normed_two_grad = reduce_tokens(norm_two_rows, local_rows)
    mid_part, gain_ffn_grad = norm_backward(
        residual_mid, factor_two, gain_ffn_f, normed_two_grad, D
    )
    mid_grad = upstream + mid_part
    attn_grad_all = gather_tokens(mid_grad.astype(jnp.bfloat16))
    grad_output = contract_rows(gated_all, attn_grad_all)
    gated_grad = share_features(contract_cols(attn_grad_all, w_output))
    head_grad = gated_grad * outgate_act
    outgate_slope = outgate_sig * (1.0 + outgate_share * (1.0 - outgate_sig))
    outgate_grad = (gated_grad * normed_head * outgate_slope).astype(jnp.bfloat16)
    mixed_grad, gain_head_grad = norm_backward(
        mixed_share, factor_head, gain_head_f, head_grad, HEAD_V
    )
    mixed_grad_all, outgate_grad_all = gather_features(
        (mixed_grad.astype(jnp.bfloat16), outgate_grad)
    )
    scaled_grad, key_grad, value_part, decay_grad = attend_back(mixed_grad_all.astype(jnp.float32))
    value_grad = lax.psum(value_part, "row").astype(jnp.bfloat16)
    query_grad = (scaled_grad * query_scale).astype(jnp.bfloat16)
    key_grad_low = key_grad.astype(jnp.bfloat16)
    logit_grad = decay_grad * jax.nn.sigmoid(-decay_logits) / 16.0
    rank_up_part = lax.dot_general(
        rank_low.astype(jnp.float32),
        logit_grad,
        (((0,), (0,)), ((), ())),
        precision=HIGHEST,
        preferred_element_type=jnp.float32,
    )
    rank_up_grad = lax.dynamic_update_slice_in_dim(
        jnp.zeros(rank_up.shape, jnp.float32), rank_up_part, row_index * key_share, 1
    )
    bias_grad = lax.dynamic_update_slice_in_dim(
        jnp.zeros(decay_bias.shape, jnp.float32),
        jnp.sum(logit_grad, axis=0),
        row_index * key_share,
        0,
    )
    rank_term = lax.dot_general(
        logit_grad,
        rank_cols.astype(jnp.float32),
        (((1,), (1,)), ((), ())),
        precision=HIGHEST,
        preferred_element_type=jnp.float32,
    )
    rank_grad = lax.psum(rank_term, ("row", "col")).astype(jnp.bfloat16)
    query_grad_all, key_grad_all = gather_features((query_grad, key_grad_low))
    grad_query = contract_rows(tokens_one, query_grad_all)
    grad_key = contract_rows(tokens_one, key_grad_all)
    grad_value = contract_rows(tokens_one, value_grad)
    grad_outgate = contract_rows(tokens_one, outgate_grad_all)
    grad_rank_down = contract_rows(tokens_one, rank_grad)

    def norm_one_rows(first_row, row_count):
        summed = contract_cols(query_grad_all, w_query)
        summed = summed + contract_cols(key_grad_all, w_key)
        summed = summed + contract_cols(value_grad, w_value)
        summed = summed + contract_cols(outgate_grad_all, w_outgate)
        return summed

    normed_one_grad = reduce_tokens(norm_one_rows, local_rows)
    own_rank = lax.dynamic_slice_in_dim(rank_grad, col_index * local_rows, local_rows, 0)
    normed_one_grad = normed_one_grad + contract_cols(own_rank, rank_down)
    input_part, gain_attn_grad = norm_backward(
        residual_in, factor_one, gain_attn_f, normed_one_grad, D
    )
    grad_input = mid_grad + input_part
    weights_summed = (
        lax.psum(grad_query.astype(jnp.bfloat16), "dp").astype(jnp.float32),
        lax.psum(grad_key.astype(jnp.bfloat16), "dp").astype(jnp.float32),
        lax.psum(grad_value.astype(jnp.bfloat16), "dp").astype(jnp.float32),
        lax.psum(grad_outgate.astype(jnp.bfloat16), "dp").astype(jnp.float32),
        lax.psum(grad_rank_down.astype(jnp.bfloat16), "dp").astype(jnp.float32),
        lax.psum(grad_output.astype(jnp.bfloat16), "dp").astype(jnp.float32),
        lax.psum(grad_gate.astype(jnp.bfloat16), "dp").astype(jnp.float32),
        lax.psum(grad_up.astype(jnp.bfloat16), "dp").astype(jnp.float32),
        lax.psum(grad_down.astype(jnp.bfloat16), "dp").astype(jnp.float32),
    )
    gains_summed = lax.psum((gain_attn_grad, gain_head_grad, gain_ffn_grad), ("dp", "col"))
    decay_summed = (
        lax.psum(rank_up_grad.astype(jnp.bfloat16), ("dp", "row")).astype(jnp.float32),
        lax.psum(bias_grad.astype(jnp.bfloat16), ("dp", "row")).astype(jnp.float32),
    )
    return (
        block_out,
        grad_input,
        gains_summed[0],
        weights_summed[0],
        weights_summed[1],
        weights_summed[2],
        weights_summed[3],
        weights_summed[4],
        decay_summed[0],
        decay_summed[1],
        gains_summed[1],
        weights_summed[5],
        gains_summed[2],
        weights_summed[6],
        weights_summed[7],
        weights_summed[8],
    )


def solution(mesh):
    placed = (
        P(("dp", "col"), "row"),
        P("dp"),
        P("row"),
        P("row", "col"),
        P("row", "col"),
        P("row", "col"),
        P("row", "col"),
        P("row", None),
        P(None, "col"),
        P("col"),
        P("row"),
        P("col", "row"),
        P("row"),
        P("row", "col"),
        P("row", "col"),
        P("col", "row"),
        P(("dp", "col"), "row"),
    )
    return jax.shard_map(
        body,
        mesh=mesh,
        in_specs=placed,
        out_specs=(
            P(("dp", "col"), "row"),
            P(("dp", "col"), "row"),
            P("row"),
            P("row", "col"),
            P("row", "col"),
            P("row", "col"),
            P("row", "col"),
            P("row", None),
            P(None, "col"),
            P("col"),
            P("row"),
            P("col", "row"),
            P("row"),
            P("row", "col"),
            P("row", "col"),
            P("col", "row"),
        ),
        check_vma=False,
    )
```

profile of v0, /device:TPU:0, one launch (start us, length us, event | category | flops | bytes accessed | tf_op | source)
XLA Modules:
  0.0 2069.8 jit_solution(14009256386679125751)
XLA Ops:
  8.7 5.8 psum.168
  18.1 56.7 %all-gather.13.cloned.1.call-done = bf16[1280,1024]{1,0:T(8,128)(2,1)} async-done(((bf16[320,1024]{1,0:T(8,128)(2,1)}), bf16[1280,1024]{1,0:T(8,128)(2,1)}) %all-gather.13.cloned.1.call-update) | async-done | bytes 2621456 | tf_op jit(solution)/shard_map/all_gather | solution.py:91
  74.8 5.0 fusion.76
  79.9 5.0 fusion.78
  85.7 5.2 fusion.79
  91.7 112.6 %all-reduce.10 = (bf16[1280,16]{0,1:T(8,128)(2,1)}, bf16[1280,512]{1,0:T(8,128)(2,1)}) all-reduce(f32[1280,16]{0,1:T(8,128)S(1)} %fusion.77, f32[1280,512]{1,0:T(8,128)} %fusion.79), channel_id=1, replica_groups=mesh['dp'=4,'row'=2,'col'=4] {'row'}, use_global_device_ids=true, to_apply=%region_3.4 | all-reduce | flops 675840 | bytes 4055040 | tf_op jit(solution)/shard_map/psum | solution.py:155
  215.7 7.2 convolution_bitcast_fusion.1
  222.9 5.2 broadcast.104.clone
  228.1 51.8 %while.34 = (s32[]{:T(128)}, f32[1,256,512]{2,1,0:T(8,128)S(1)}, f32[20,1,256,512]{3,2,1,0:T(8,128)}, f32[20,1,256,1]{2,3,1,0:T(1,128)}, f32[20,1,256]{2,1,0:T(1...) while((s32[]{:T(128)}, f32[1,256,512]{2,1,0:T(8,128)S(1)}, ...), condition=%wide.region_8.9_spmd.clone, body=%wide.region_7.8_spmd.clone.sunk | while | flops 524291 | bytes 2627688 | solution.py:64
  285.1 12.0 fusion.10
  297.6 5.0 fusion.81
  303.3 32.6 %reduce-scatter.17.cloned.1.call-done = f32[1280,256]{1,0:T(8,128)} async-done(((f32[1280,512]{1,0:T(8,128)}), f32[1280,256]{1,0:T(8,128)}) %reduce-scatter.17.cloned.1.call-update) | async-done | bytes 1310736 | tf_op jit(solution)/shard_map/reduce_scatter | solution.py:95
  337.5 5.0 psum.171
  342.5 33.8 %reduce-scatter.19.cloned.1.call-done = f32[1280,256]{1,0:T(8,128)} async-done(((f32[1280,512]{1,0:T(8,128)}), f32[1280,256]{1,0:T(8,128)}) %reduce-scatter.19.cloned.1.call-update) | async-done | bytes 1310736 | tf_op jit(solution)/shard_map/reduce_scatter | solution.py:95
  379.4 24.3 %all-gather.15.cloned.1.call-done = bf16[1280,512]{1,0:T(8,128)(2,1)} async-done(((bf16[1280,256]{1,0:T(8,128)(2,1)}), bf16[1280,512]{1,0:T(8,128)(2,1)}) %all-gather.15.cloned.1.call-update) | async-done | bytes 1310736 | tf_op jit(solution)/shard_map/all_gather | solution.py:101
  403.7 5.5 fusion.82
  414.1 89.1 %reduce-scatter.21.cloned.1.call-done = f32[320,1024]{1,0:T(8,128)} async-done(((f32[1280,1024]{1,0:T(8,128)}), f32[320,1024]{1,0:T(8,128)}) %reduce-scatter.21.cloned.1.call-update) | async-done | bytes 1310736 | tf_op jit(solution)/shard_map/reduce_scatter | solution.py:107
  506.3 5.0 psum.172
  514.4 46.3 %all-gather.21.cloned.1.call-done = bf16[1280,1024]{1,0:T(8,128)(2,1)} async-done(((bf16[320,1024]{1,0:T(8,128)(2,1)}), bf16[1280,1024]{1,0:T(8,128)(2,1)}) %all-gather.21.cloned.1.call-update) | async-done | bytes 2621456 | tf_op jit(solution)/shard_map/all_gather | solution.py:91
  560.7 9.5 fusion.86
  570.2 46.2 %all-gather.17.cloned.1.call-done = bf16[1280,1024]{1,0:T(8,128)(2,1)} async-done(((bf16[320,1024]{1,0:T(8,128)(2,1)}), bf16[1280,1024]{1,0:T(8,128)(2,1)}) %all-gather.17.cloned.1.call-update) | async-done | bytes 2621456 | tf_op jit(solution)/shard_map/all_gather | solution.py:91
  616.4 8.3 fusion.83
  624.8 9.5 fusion.84
  634.4 70.0 %reduce-scatter.29.cloned.1.call-done = f32[1280,704]{0,1:T(8,128)} async-done(((f32[1280,1408]{0,1:T(8,128)}), f32[1280,704]{0,1:T(8,128)}) %reduce-scatter.29.cloned.1.call-update) | async-done | bytes 3604496 | tf_op jit(solution)/shard_map/reduce_scatter | solution.py:95
  704.4 89.5 %reduce-scatter.23.cloned.1.call-done = f32[1280,704]{0,1:T(8,128)} async-done(((f32[1280,1408]{0,1:T(8,128)}), f32[1280,704]{0,1:T(8,128)}) %reduce-scatter.23.cloned.1.call-update) | async-done | bytes 3604496 | tf_op jit(solution)/shard_map/reduce_scatter | solution.py:95
  793.9 89.2 %reduce-scatter.25.cloned.1.call-done = f32[1280,704]{0,1:T(8,128)} async-done(((f32[1280,1408]{0,1:T(8,128)}), f32[1280,704]{0,1:T(8,128)}) %reduce-scatter.25.cloned.1.call-update) | async-done | bytes 3604496 | tf_op jit(solution)/shard_map/reduce_scatter | solution.py:95
  883.1 6.6 multiply_convert_fusion
  891.1 48.9 %all-gather.23.cloned.1.call-done = bf16[1280,1408]{0,1:T(8,128)(2,1)} async-done(((bf16[1280,704]{0,1:T(8,128)(2,1)}), bf16[1280,1408]{0,1:T(8,128)(2,1)}) %all-gather.23.cloned.1.call-update) | async-done | bytes 3604496 | tf_op jit(solution)/shard_map/all_gather | solution.py:101
  940.0 8.0 fusion.87
  948.1 44.1 %all-gather.25.cloned.1.call-done = bf16[1280,1408]{0,1:T(8,128)(2,1)} async-done(((bf16[1280,704]{0,1:T(8,128)(2,1)}), bf16[1280,1408]{0,1:T(8,128)(2,1)}) %all-gather.25.cloned.1.call-update) | async-done | bytes 3604496 | tf_op jit(solution)/shard_map/all_gather | solution.py:101
  992.2 11.2 convolution_add_fusion
  1003.4 40.9 %all-gather.19.cloned.1.call-done = bf16[1280,1408]{0,1:T(8,128)(2,1)} async-done(((bf16[1280,704]{0,1:T(8,128)(2,1)}), bf16[1280,1408]{0,1:T(8,128)(2,1)}) %all-gather.19.cloned.1.call-update) | async-done | bytes 3604496 | tf_op jit(solution)/shard_map/all_gather | solution.py:101
  1044.4 8.0 fusion.85
  1052.5 88.5 %reduce-scatter.31.cloned.1.call-done = f32[320,1024]{1,0:T(8,128)} async-done(((f32[1280,1024]{1,0:T(8,128)}), f32[320,1024]{1,0:T(8,128)}) %reduce-scatter.31.cloned.1.call-update) | async-done | bytes 1310736 | tf_op jit(solution)/shard_map/reduce_scatter | solution.py:107
  1143.4 4.9 psum.173
  1148.3 89.8 %reduce-scatter.27.cloned.1.call-done = f32[320,1024]{1,0:T(8,128)} async-done(((f32[1280,1024]{1,0:T(8,128)}), f32[320,1024]{1,0:T(8,128)}) %reduce-scatter.27.cloned.1.call-update) | async-done | bytes 1310736 | tf_op jit(solution)/shard_map/reduce_scatter | solution.py:107
  1241.6 55.5 %all-gather.27.cloned.1.call-done = bf16[1280,1024]{1,0:T(8,128)(2,1)} async-done(((bf16[320,1024]{1,0:T(8,128)(2,1)}), bf16[1280,1024]{1,0:T(8,128)(2,1)}) %all-gather.27.cloned.1.call-update) | async-done | bytes 2621456 | tf_op jit(solution)/shard_map/all_gather | solution.py:91
  1297.0 5.1 fusion.88
  1303.8 7.8 convolution_convert_fusion.1
  1311.6 5.7 convolution_convert_fusion.2
  1317.3 21.3 %reduce-scatter.33.cloned.1.call-done = f32[1280,256]{1,0:T(8,128)} async-done(((f32[1280,512]{1,0:T(8,128)}), f32[1280,256]{1,0:T(8,128)}) %reduce-scatter.33.cloned.1.call-update) | async-done | bytes 1310736 | tf_op jit(solution)/shard_map/reduce_scatter | solution.py:95
  1342.2 5.0 psum.174
  1350.0 8.5 convolution_convert_fusion
  1361.4 12.9 all-gather.29.cloned.1.call-done
  1374.3 9.8 convolution_bitcast_fusion
  1384.1 10.8 fusion.5
  1397.5 5.3 broadcast.104
  1402.9 136.7 %while.35 = (s32[]{:T(128)}, f32[1,256,512]{2,1,0:T(8,128)S(1)}, f32[20,1,256,512]{3,2,1,0:T(8,128)}, f32[20,1,256]{2,1,0:T(1,128)S(1)}, f32[20,1,256,512]{2,3,0...) while((s32[]{:T(128)}, f32[1,256,512]{2,1,0:T(8,128)S(1)}, ...), condition=%wide.region_28.29_spmd.clone, body=%wide.region_26.28_spmd.clone.sunk | while | flops 786180 | bytes 5249168 | solution.py:64
  1539.7 10.9 fusion.50
  1550.6 9.8 fusion.13
  1568.0 78.9 %all-reduce.11 = bf16[1280,512]{1,0:T(8,128)(2,1)} all-reduce(f32[1280,512]{1,0:T(8,128)} %bitcast.223), channel_id=1, replica_groups=mesh['dp'=4,'row'=2,'col'=4] {'row'}, use_global_device_ids=true, to_apply=%region_29.30 | all-reduce | flops 655360 | bytes 3932160 | tf_op jit(solution)/shard_map/psum | solution.py:244
  1647.1 3.8 convolution_convert_fusion.5
  1654.7 3.9 convolution_convert_fusion.6
  1658.6 13.4 all-gather.31.cloned.1.call-done
  1672.0 3.8 convolution_convert_fusion.7
  1683.8 4.2 add_add_fusion
  1694.1 23.7 %all-reduce.3 = (bf16[16,512]{1,0:T(8,128)(2,1)S(1)}, bf16[512]{0:T(512)(128)(2,1)S(1)}) all-reduce(bf16[16,512]{1,0:T(8,128)(2,1)S(1)} %convolution_dynamic-update-slice_fusion, bf16[512]{0:T(512)(128)(2,1)S(1)} %dynamic_update_slice.34), channel_id=1, replica_groups=mesh['dp'=4,'row'=2,'col'=4] {'dp','row'}, use_global_device_ids=true, to_apply=%region_43.44 | all-reduce | flops 8704 | bytes 34816 | tf_op jit(solution)/shard_map/psum | solution.py:306
  1719.8 38.8 %psum.176 = bf16[1280,16]{0,1:T(8,128)(2,1)S(1)} all-reduce(f32[1280,16]{0,1:T(8,128)S(1)} %fusion.60), channel_id=1, replica_groups=mesh['dp'=4,'row'=2,'col'=4] {'row','col'}, use_global_device_ids=true, to_apply=%region_33.34 | all-reduce | flops 20480 | bytes 122880 | tf_op jit(solution)/shard_map/psum | solution.py:271
  1760.8 12.6 psum.183
  1774.0 147.4 %all-reduce.9.cloned.1.call-done = (bf16[1024,512]{1,0:T(8,128)(2,1)}, bf16[1024,512]{1,0:T(8,128)(2,1)}, bf16[1024,512]{1,0:T(8,128)(2,1)}, bf16[1024,512]{1,0:...) async-done(((bf16[1024,512]{1,0:T(8,128)(2,1)}, bf16[1024,512]{1,0:T(8,128)(2,1)}, ...) | async-done | bytes 13893648 | tf_op jit(solution)/shard_map/psum | solution.py:294
  1921.4 4.9 convert_element_type.203
  1940.8 76.9 %reduce-scatter.35.cloned.1.call-done = f32[320,1024]{1,0:T(8,128)} async-done(((f32[1280,1024]{1,0:T(8,128)}), f32[320,1024]{1,0:T(8,128)}) %reduce-scatter.35.cloned.1.call-update) | async-done | bytes 1310736 | tf_op jit(solution)/shard_map/reduce_scatter | solution.py:107
  2020.7 4.9 psum.177
  2025.7 33.8 %all-reduce.1 = (f32[1024]{0:T(1024)}, f32[256]{0:T(256)}, f32[1024]{0:T(1024)}) all-reduce(f32[1024]{0:T(1024)S(1)} %get-tuple-element.257, f32[256]{0:T(256)S(1)} %copy-done.72, f32[1024]{0:T(1024)S(1)} %copy-done.67), channel_id=1, replica_groups=mesh['dp'=4,'row'=2,'col'=4] {'dp','col'}, use_global_device_ids=true, to_apply=%region_37.38 | all-reduce | flops 2304 | bytes 18432 | tf_op jit(solution)/shard_map/psum | solution.py:304
  (490 shorter events, 298.9 us)
Async XLA Ops:
  7.2 609.2 %copy-start = (bf16[1024,1408]{1,0:T(8,128)(2,1)S(1)}, bf16[1024,1408]{1,0:T(8,128)(2,1)}, u32[]{:S(2)}) copy-start(bf16[1024,1408]{1,0:T(8,128)(2,1)} %param.34) | copy-start | bytes 8650756
  7.2 67.6 %all-gather.13.cloned.1.call-start = ((), (), s32[]{:S(2)}) async-start(), calls=%async_computation.12 | async-start | bytes 3276800 | tf_op jit(solution)/shard_map/all_gather | solution.py:91
  14.5 65.3 %copy-start.63 = (f32[320]{0:T(512)}, f32[320]{0:T(512)S(1)}, u32[]{:S(2)}) copy-start(f32[320]{0:T(512)S(1)} %psum.168) | copy-start | bytes 3844
  18.0 191.0 %reduce-scatter.13.cloned.1.call-start = ((), (), s32[]{:S(2)}) async-start(), calls=%async_computation.13 | async-start | bytes 3932160 | tf_op jit(solution)/shard_map/reduce_scatter | solution.py:95
  79.8 133.7 %reduce-scatter.15.cloned.1.call-start = ((), (), s32[]{:S(2)}) async-start(), calls=%async_computation.14 | async-start | bytes 3932160 | tf_op jit(solution)/shard_map/reduce_scatter | solution.py:95
  84.9 251.0 %reduce-scatter.17.cloned.1.call-start = ((), (), s32[]{:S(2)}) async-start(), calls=%async_computation.15 | async-start | bytes 3932160 | tf_op jit(solution)/shard_map/reduce_scatter | solution.py:95
  85.7 194.2 %copy-start.48 = (f32[64,64]{1,0:T(8,128)}, f32[64,64]{1,0:T(8,128)S(1)}, u32[]{:S(2)}) copy-start(f32[64,64]{1,0:T(8,128)S(1)} %fusion.52) | copy-start | bytes 49156
  91.7 112.6 %copy-start.70 = (bf16[16,512]{1,0:T(8,128)(2,1)S(1)}, bf16[16,512]{1,0:T(8,128)(2,1)}, u32[]{:S(2)}) copy-start(bf16[16,512]{1,0:T(8,128)(2,1)} %param.29) | copy-start | bytes 49156
  297.1 79.2 %reduce-scatter.19.cloned.1.call-start = ((), (), s32[]{:S(2)}) async-start(), calls=%async_computation.16 | async-start | bytes 3932160 | tf_op jit(solution)/shard_map/reduce_scatter | solution.py:95
  302.7 101.0 %all-gather.15.cloned.1.call-start = ((), (), s32[]{:S(2)}) async-start(), calls=%async_computation.17 | async-start | bytes 1966080 | tf_op jit(solution)/shard_map/all_gather | solution.py:101
  303.3 76.0 %copy-start.68 = (f32[256]{0:T(256)}, f32[256]{0:T(256)S(1)}, u32[]{:S(2)}) copy-start(f32[256]{0:T(256)S(1)} %convert_element_type.167) | copy-start | bytes 3076
  379.3 123.8 %reduce-scatter.21.cloned.1.call-start = ((), (), s32[]{:S(2)}) async-start(), calls=%async_computation.18 | async-start | bytes 6553600 | tf_op jit(solution)/shard_map/reduce_scatter | solution.py:107
  409.2 93.9 %copy-start.18 = (bf16[320,1024]{1,0:T(8,128)(2,1)S(1)}, bf16[320,1024]{1,0:T(8,128)(2,1)}, u32[]{:S(2)}) copy-start(bf16[320,1024]{1,0:T(8,128)(2,1)} %param.21) | copy-start | bytes 1966084
  409.2 151.4 %all-gather.21.cloned.1.call-start = ((), (), s32[]{:S(2)}) async-start(), calls=%async_computation.24 | async-start | bytes 3276800 | tf_op jit(solution)/shard_map/all_gather | solution.py:91
  412.7 203.7 %all-gather.17.cloned.1.call-start = ((), (), s32[]{:S(2)}) async-start(), calls=%async_computation.19 | async-start | bytes 3276800 | tf_op jit(solution)/shard_map/all_gather | solution.py:91
  514.4 190.0 %reduce-scatter.29.cloned.1.call-start = ((), (), s32[]{:S(2)}) async-start(), calls=%async_computation.25 | async-start | bytes 10813440 | tf_op jit(solution)/shard_map/reduce_scatter | solution.py:95
  570.2 223.7 %reduce-scatter.23.cloned.1.call-start = ((), (), s32[]{:S(2)}) async-start(), calls=%async_computation.20 | async-start | bytes 10813440 | tf_op jit(solution)/shard_map/reduce_scatter | solution.py:95
  624.7 258.3 %reduce-scatter.25.cloned.1.call-start = ((), (), s32[]{:S(2)}) async-start(), calls=%async_computation.21 | async-start | bytes 10813440 | tf_op jit(solution)/shard_map/reduce_scatter | solution.py:95
  634.3 305.7 %all-gather.23.cloned.1.call-start = ((), (), s32[]{:S(2)}) async-start(), calls=%async_computation.26 | async-start | bytes 5406720 | tf_op jit(solution)/shard_map/all_gather | solution.py:101
  889.7 102.5 %all-gather.25.cloned.1.call-start = ((), (), s32[]{:S(2)}) async-start(), calls=%async_computation.27 | async-start | bytes 5406720 | tf_op jit(solution)/shard_map/all_gather | solution.py:101
  890.3 154.1 %all-gather.19.cloned.1.call-start = ((), (), s32[]{:S(2)}) async-start(), calls=%async_computation.22 | async-start | bytes 5406720 | tf_op jit(solution)/shard_map/all_gather | solution.py:101
  890.9 250.1 %reduce-scatter.31.cloned.1.call-start = ((), (), s32[]{:S(2)}) async-start(), calls=%async_computation.28 | async-start | bytes 6553600 | tf_op jit(solution)/shard_map/reduce_scatter | solution.py:107
  1003.4 41.0 %copy-start.75 = (bf16[1408,1024]{1,0:T(8,128)(2,1)S(1)}, bf16[1408,1024]{1,0:T(8,128)(2,1)}, u32[]{:S(2)}) copy-start(bf16[1408,1024]{1,0:T(8,128)(2,1)} %param.36) | copy-start | bytes 8650756
  1003.4 234.8 %reduce-scatter.27.cloned.1.call-start = ((), (), s32[]{:S(2)}) async-start(), calls=%async_computation.23 | async-start | bytes 6553600 | tf_op jit(solution)/shard_map/reduce_scatter | solution.py:107
  1052.4 88.6 %copy-start.17 = (f32[320,1024]{1,0:T(8,128)S(1)}, f32[320,1024]{1,0:T(8,128)}, u32[]{:S(2)}) copy-start(f32[320,1024]{1,0:T(8,128)} %get-tuple-element.305) | copy-start | bytes 3932164
  1052.4 88.6 %copy-start.53 = (f32[1024]{0:T(1024)S(1)}, f32[1024]{0:T(1024)}, u32[]{:S(2)}) copy-start(f32[1024]{0:T(1024)} %convert_element_type.169) | copy-start | bytes 12292
  1052.4 88.6 %copy-start.58 = (f32[320]{0:T(512)S(1)}, f32[320]{0:T(512)}, u32[]{:S(2)}) copy-start(f32[320]{0:T(512)} %copy-done.57) | copy-start | bytes 3844
  1052.4 95.9 %copy-start.66 = (f32[320]{0:T(512)S(1)}, f32[320]{0:T(512)}, u32[]{:S(2)}) copy-start(f32[320]{0:T(512)} %copy-done.65) | copy-start | bytes 3844
  1052.4 185.7 %copy-start.34 = (bf16[320,1024]{1,0:T(8,128)(2,1)S(1)}, bf16[320,1024]{1,0:T(8,128)(2,1)}, u32[]{:S(2)}) copy-start(bf16[320,1024]{1,0:T(8,128)(2,1)} %param.37) | copy-start | bytes 1966084
  1052.4 185.7 %copy-start.62 = (f32[320]{0:T(512)S(1)}, f32[320]{0:T(512)}, u32[]{:S(2)}) copy-start(f32[320]{0:T(512)} %copy-done.61) | copy-start | bytes 3844
  1052.5 244.5 %all-gather.27.cloned.1.call-start = ((), (), s32[]{:S(2)}) async-start(), calls=%async_computation.29 | async-start | bytes 3276800 | tf_op jit(solution)/shard_map/all_gather | solution.py:91
  1141.0 97.1 %copy-start.30 = (f32[320,1024]{1,0:T(8,128)S(1)}, f32[320,1024]{1,0:T(8,128)}, u32[]{:S(2)}) copy-start(f32[320,1024]{1,0:T(8,128)} %reduce-scatter.31.cloned.1.call-done) | copy-start | bytes 3932164
  1241.5 97.1 %reduce-scatter.33.cloned.1.call-start = ((), (), s32[]{:S(2)}) async-start(), calls=%async_computation.30 | async-start | bytes 3932160 | tf_op jit(solution)/shard_map/reduce_scatter | solution.py:95
  1302.1 72.2 %all-gather.29.cloned.1.call-start = ((), (), s32[]{:S(2)}) async-start(), calls=%async_computation.31 | async-start | bytes 1966080 | tf_op jit(solution)/shard_map/all_gather | solution.py:101
  1303.8 7.8 copy-start.77
  1311.6 27.0 %copy-start.16 = (f32[1280,256]{1,0:T(8,128)S(1)}, f32[1280,256]{1,0:T(8,128)}, u32[]{:S(2)}) copy-start(f32[1280,256]{1,0:T(8,128)} %reduce-scatter.17.cloned.1.call-done) | copy-start | bytes 3932164
  1311.6 27.0 %copy-start.22 = (f32[1280,256]{1,0:T(8,128)S(1)}, f32[1280,256]{1,0:T(8,128)}, u32[]{:S(2)}) copy-start(f32[1280,256]{1,0:T(8,128)} %reduce-scatter.19.cloned.1.call-done) | copy-start | bytes 3932164
  1311.6 27.0 %copy-start.69 = (f32[256]{0:T(256)S(1)}, f32[256]{0:T(256)}, u32[]{:S(2)}) copy-start(f32[256]{0:T(256)} %copy-done.68) | copy-start | bytes 3076
  1349.9 8.5 copy-start.38
  1349.9 301.0 %all-gather.35.cloned.1.call-start = ((), (), s32[]{:S(2)}) async-start(), calls=%async_computation.34 | async-start | bytes 1966080 | tf_op jit(solution)/shard_map/all_gather | solution.py:101
  1350.0 8.5 copy-start.35
  1358.4 15.9 copy-start.9
  1361.0 293.8 %all-gather.33.cloned.1.call-start = ((), (), s32[]{:S(2)}) async-start(), calls=%async_computation.33 | async-start | bytes 1966080 | tf_op jit(solution)/shard_map/all_gather | solution.py:101
  1374.3 9.8 copy-start.14
  1384.1 10.8 copy-start.27
  1402.8 136.8 %copy-start.4 = (f32[1280,256]{1,0:T(8,128)S(1)}, f32[1280,256]{1,0:T(8,128)}, u32[]{:S(2)}) copy-start(f32[1280,256]{1,0:T(8,128)} %copy-done.3) | copy-start | bytes 3932164
  1402.9 136.8 %copy-start.7 = (f32[1,20,64,256]{3,2,1,0:T(8,128)S(1)}, f32[1,20,64,256]{3,2,1,0:T(8,128)}, u32[]{:S(2)}) copy-start(f32[1,20,64,256]{3,2,1,0:T(8,128)} %copy-done.5) | copy-start | bytes 3932164
  1402.9 136.8 %copy-start.47 = (f32[1,20,1,256]{3,1,2,0:T(8,128)S(1)}, f32[1,20,1,256]{3,1,2,0:T(8,128)}, u32[]{:S(2)}) copy-start(f32[1,20,1,256]{3,1,2,0:T(8,128)} %copy-done.46) | copy-start | bytes 61444
  1539.6 11.0 copy-start.2
  1550.6 9.9 copy-start.13
  1550.6 9.9 copy-start.15
  1550.6 9.9 copy-start.49
  1568.0 79.1 %copy-start.24 = (bf16[1280,1024]{1,0:T(8,128)(2,1)S(1)}, bf16[1280,1024]{1,0:T(8,128)(2,1)}, u32[]{:S(2)}) copy-start(bf16[1280,1024]{1,0:T(8,128)(2,1)} %all-gather.13.cloned.1.call-done) | copy-start | bytes 7864324
  1568.0 104.0 %all-gather.31.cloned.1.call-start = ((), (), s32[]{:S(2)}) async-start(), calls=%async_computation.32 | async-start | bytes 1966080 | tf_op jit(solution)/shard_map/all_gather | solution.py:101
  1647.0 274.4 %all-reduce.9.cloned.1.call-start = ((), (), s32[]{:S(2)}) async-start(), calls=%async_computation.36 | async-start | bytes 27787264 | tf_op jit(solution)/shard_map/psum | solution.py:294
  1675.9 341.8 %reduce-scatter.35.cloned.1.call-start = ((), (), s32[]{:S(2)}) async-start(), calls=%async_computation.35 | async-start | bytes 6553600 | tf_op jit(solution)/shard_map/reduce_scatter | solution.py:107
  1693.2 25.8 %copy-start.71 = (bf16[16,512]{1,0:T(8,128)(2,1)S(1)}, bf16[16,512]{1,0:T(8,128)(2,1)}, u32[]{:S(2)}) copy-start(bf16[16,512]{1,0:T(8,128)(2,1)} %param.29) | copy-start | bytes 49156
  1939.2 78.5 %copy-start.19 = (bf16[320,1024]{1,0:T(8,128)(2,1)S(1)}, bf16[320,1024]{1,0:T(8,128)(2,1)}, u32[]{:S(2)}) copy-start(bf16[320,1024]{1,0:T(8,128)(2,1)} %param.21) | copy-start | bytes 1966084
  1939.2 78.5 %copy-start.52 = (bf16[1024,16]{0,1:T(8,128)(2,1)S(1)}, bf16[1024,16]{0,1:T(8,128)(2,1)}, u32[]{:S(2)}) copy-start(bf16[1024,16]{0,1:T(8,128)(2,1)} %param.28) | copy-start | bytes 98308
  1939.2 78.5 %copy-start.55 = (f32[1024]{0:T(1024)S(1)}, f32[1024]{0:T(1024)}, u32[]{:S(2)}) copy-start(f32[1024]{0:T(1024)} %copy-done.54) | copy-start | bytes 12292
  1939.2 78.5 %copy-start.60 = (f32[320]{0:T(512)S(1)}, f32[320]{0:T(512)}, u32[]{:S(2)}) copy-start(f32[320]{0:T(512)} %copy-done.59) | copy-start | bytes 3844
  1940.8 84.9 %copy-start.64 = (f32[320]{0:T(512)S(1)}, f32[320]{0:T(512)}, u32[]{:S(2)}) copy-start(f32[320]{0:T(512)} %copy-done.63) | copy-start | bytes 3844
  1940.8 84.9 %copy-start.67 = (f32[1024]{0:T(1024)S(1)}, f32[1024]{0:T(1024)}, u32[]{:S(2)}) copy-start(f32[1024]{0:T(1024)} %get-tuple-element.255) | copy-start | bytes 12292
  1940.8 84.9 %copy-start.72 = (f32[256]{0:T(256)S(1)}, f32[256]{0:T(256)}, u32[]{:S(2)}) copy-start(f32[256]{0:T(256)} %get-tuple-element.253) | copy-start | bytes 3076
  (44 other events, 101.8 us)
Sparse Core Ops, SparseCore 0:
  18.1 56.6 all-gather.12
  79.9 53.6 reduce-scatter.12
  136.6 66.5 reduce-scatter.14
  297.3 38.6 reduce-scatter.16
  338.7 37.5 reduce-scatter.18
  379.4 24.1 all-gather.14
  409.3 93.7 reduce-scatter.20
  505.3 55.3 all-gather.20
  562.8 53.5 all-gather.16
  618.6 85.7 reduce-scatter.28
  706.8 87.0 reduce-scatter.22
  796.0 86.9 reduce-scatter.24
  889.9 50.1 all-gather.22
  942.1 50.0 all-gather.24
  994.2 50.0 all-gather.18
  1047.2 93.7 reduce-scatter.30
  1143.8 94.2 reduce-scatter.26
  1241.6 55.3 all-gather.26
  1302.2 36.3 reduce-scatter.32
  1350.0 24.2 all-gather.28
  1376.4 24.2 all-gather.34
  1568.1 38.4 all-gather.32
  1647.1 24.8 all-gather.30
  1676.2 245.1 all-reduce.8
  1923.7 93.9 reduce-scatter.34
where the time goes:
time: 2080 us; the launch traced here: 2070 us
  waiting for transfers between devices  1220 us (59%)
  blocking collectives  331 us (16%)
  matrix products  220 us (11%)
  other arithmetic  154 us (7%)
  local copies, waits for them, and re-layouts  126 us (6%)
    reduce_scatter x4, waiting for transfers between devices, reduce_tokens(): lax.psum_scatter(builder(jnp.int32(0), local_rows * lax.axis_size('col'))...  344 us
    reduce_scatter x8, waiting for transfers between devices, share_features(): return lax.psum_scatter(parts, 'row', scatter_dimension=1, tiled=True)  336 us
    all_gather x4, waiting for transfers between devices, gather_tokens(): return lax.all_gather(tensor, 'col', axis=0, tiled=True)  205 us
    all_gather x8, waiting for transfers between devices, gather_features(): lax.all_gather(for_sending(parts), 'row', axis=1, tiled=True)  185 us
    psum x1, waiting for transfers between devices, body(): lax.psum(grad_query.astype(jnp.bfloat16), 'dp').astype(jnp.float32)  147 us
    psum x1, blocking collectives, body(): lax.psum((product(tokens_one, w_value), product(tokens_one, rank_down)),...  113 us
    dynamic_slice x80, local copies, waits for them, and re-layouts, gla_sequence(): _, earlier = lax.scan(advance, initial, (updates, fading))  91.4 us
    psum x1, blocking collectives, body(): value_grad = lax.psum(value_part, 'row').astype(jnp.bfloat16)  78.9 us
  transfers between devices with their start and end apart: 25, of which 21 were waited for; matrix products, arithmetic and copies ran while one was open for 17% of the time, Pallas kernels for 0%

commit v1 on v0

--- a/solution.py
+++ b/solution.py
@@ -1,8 +1,10 @@
+import functools
 import math
 import jax
 import jax.numpy as jnp
 from jax import lax
 from jax.sharding import PartitionSpec as P
+from jax.lax import axis_index, axis_size, ppermute
 
 D = 2048
 HEAD_K = 512
@@ -11,6 +13,36 @@
 SLOT = 1280
 EPSILON = 1e-06
 HIGHEST = lax.Precision.HIGHEST
+
+
+def switch_frames(q_in, comm_axis, at_axis):
+    prior = axis_index(comm_axis)
+    next_value = axis_size(comm_axis)
+    q_next, upper, low = (next_value, prior, q_in.shape[at_axis])
+    line_up = [(hop_no, (hop_no + 1) % q_next) for hop_no in range(q_next)]
+    row_out = jnp.zeros(
+        (*q_in.shape[:at_axis], q_next * low, *q_in.shape[at_axis + 1 :]), q_in.dtype
+    )
+    row_out = lax.dynamic_update_slice_in_dim(row_out, q_in, upper * low, axis=at_axis)
+    r2 = high = q_in
+    parts_seen = [(hop_no, (hop_no - 1) % q_next) for hop_no in range(q_next)]
+    i = 1
+    all_values = q_next // 2
+    while i < all_values + 1:
+        r2 = ppermute(r2, comm_axis, perm=line_up)
+        row_out = lax.dynamic_update_slice_in_dim(
+            row_out, r2, (upper - i) % q_next * low, axis=at_axis
+        )
+        if i < q_next - all_values:
+            high = ppermute(high, axis_name=comm_axis, perm=parts_seen)
+            row_out = lax.dynamic_update_slice_in_dim(
+                row_out, high, (upper + i) % q_next * low, axis=at_axis
+            )
+        i += 1
+    return row_out
+
+
+remake_marks_here = functools.partial(switch_frames, comm_axis="col", at_axis=0)
 
 
 def for_sending(x):
@@ -88,7 +120,7 @@
 
 
 def gather_tokens(tensor):
-    return lax.all_gather(tensor, "col", axis=0, tiled=True)
+    return remake_marks_here(tensor)
 
 
 def share_features(parts):

time: 2080 us -> 2000 us (0.962)
  waiting for transfers between devices: 1220 us -> 1080 us
  starting transfers between devices: 2.54 us -> 58.5 us
    all_gather x4 -> x0, waiting for transfers between devices: 205 us -> none  [gather_tokens(): return lax.all_gather(tensor, 'col', axis=0, tiled=True)]
    ppermute x0 -> x12, waiting for transfers between devices: none -> 163 us  [the longest x8 135 us: switch_frames(): r2 = ppermute(r2, comm_axis, perm=line_up)]
    ppermute x0 -> x12, starting transfers between devices: none -> 56.1 us  [the longest x8 46.8 us: switch_frames(): r2 = ppermute(r2, comm_axis, perm=line_up)]
    reduce_scatter x8, waiting for transfers between devices: 336 us -> 282 us  [share_features(): return lax.psum_scatter(parts, 'row', scatter_dimension=1, tiled=True)]
    reduce_scatter x4, waiting for transfers between devices: 344 us -> 299 us  [reduce_tokens(): lax.psum_scatter(builder(jnp.int32(0), local_rows * lax.axis_size('col'))...]
  transfers between devices with their start and end apart: 25 -> 33, of which waited for: 21 -> 29; matrix products, arithmetic and copies ran while one was open for 17% -> 18% of each run, Pallas kernels for 0% -> 0%
where the time goes in v1:
time: 2000 us; the launch traced here: 1990 us
  waiting for transfers between devices  1080 us (54%)
  blocking collectives  328 us (16%)
  matrix products  217 us (11%)
  other arithmetic  149 us (7%)
  local copies, waits for them, and re-layouts  140 us (7%)
  starting transfers between devices  58.5 us (3%)
    reduce_scatter x4, waiting for transfers between devices, reduce_tokens(): lax.psum_scatter(builder(jnp.int32(0), local_rows * lax.axis_size('col'))...  299 us
    reduce_scatter x8, waiting for transfers between devices, share_features(): return lax.psum_scatter(parts, 'row', scatter_dimension=1, tiled=True)  282 us
    all_gather x8, waiting for transfers between devices, gather_features(): lax.all_gather(for_sending(parts), 'row', axis=1, tiled=True)  183 us
    psum x1, waiting for transfers between devices, body(): lax.psum(grad_query.astype(jnp.bfloat16), 'dp').astype(jnp.float32)  148 us
    ppermute x8, waiting for transfers between devices, switch_frames(): r2 = ppermute(r2, comm_axis, perm=line_up)  135 us
    psum x1, blocking collectives, body(): lax.psum((product(tokens_one, w_value), product(tokens_one, rank_down)),...  110 us
    dynamic_slice x80, local copies, waits for them, and re-layouts, gla_sequence(): _, earlier = lax.scan(advance, initial, (updates, fading))  91.2 us
    psum x1, blocking collectives, body(): value_grad = lax.psum(value_part, 'row').astype(jnp.bfloat16)  78.4 us
  transfers between devices with their start and end apart: 33, of which 29 were waited for; matrix products, arithmetic and copies ran while one was open for 18% of the time, Pallas kernels for 0%

profile of v1, /device:TPU:0, one launch (start us, length us, event | category | flops | bytes accessed | tf_op | source)
XLA Modules:
  0.0 1985.0 jit_solution(16263508365924455028)
XLA Ops:
  8.7 5.8 psum.168
  22.3 15.8 collective-permute-done
  38.1 9.4 collective-permute-start.2
  52.9 11.2 collective-permute-done.2
  70.9 5.0 fusion.79
  76.7 5.2 fusion.80
  84.5 110.2 %all-reduce.10 = (bf16[1280,16]{0,1:T(8,128)(2,1)}, bf16[1280,512]{1,0:T(8,128)(2,1)}) all-reduce(f32[1280,16]{0,1:T(8,128)S(1)} %fusion.78, f32[1280,512]{1,0:T(8,128)} %fusion.80), channel_id=1, replica_groups=mesh['dp'=4,'row'=2,'col'=4] {'row'}, use_global_device_ids=true, to_apply=%region_3.4 | all-reduce | flops 675840 | bytes 4055040 | tf_op jit(solution)/shard_map/psum | solution.py:187
  206.1 7.1 convolution_bitcast_fusion.1
  213.2 5.3 broadcast.114.clone
  218.5 51.7 %while.34 = (s32[]{:T(128)}, f32[1,256,512]{2,1,0:T(8,128)S(1)}, f32[20,1,256,512]{3,2,1,0:T(8,128)}, f32[20,1,256,1]{2,3,1,0:T(1,128)}, f32[20,1,256]{2,1,0:T(1...) while((s32[]{:T(128)}, f32[1,256,512]{2,1,0:T(8,128)S(1)}, ...), condition=%wide.region_8.9_spmd.clone, body=%wide.region_7.8_spmd.clone.sunk | while | flops 524291 | bytes 2627688 | solution.py:96
  275.5 12.0 fusion.10
  288.0 5.0 fusion.82
  293.7 32.7 %reduce-scatter.17.cloned.1.call-done = f32[1280,256]{1,0:T(8,128)} async-done(((f32[1280,512]{1,0:T(8,128)}), f32[1280,256]{1,0:T(8,128)}) %reduce-scatter.17.cloned.1.call-update) | async-done | bytes 1310736 | tf_op jit(solution)/shard_map/reduce_scatter | solution.py:127
  328.0 5.0 psum.171
  333.0 33.8 %reduce-scatter.19.cloned.1.call-done = f32[1280,256]{1,0:T(8,128)} async-done(((f32[1280,512]{1,0:T(8,128)}), f32[1280,256]{1,0:T(8,128)}) %reduce-scatter.19.cloned.1.call-update) | async-done | bytes 1310736 | tf_op jit(solution)/shard_map/reduce_scatter | solution.py:127
  369.8 24.3 %all-gather.9.cloned.1.call-done = bf16[1280,512]{1,0:T(8,128)(2,1)} async-done(((bf16[1280,256]{1,0:T(8,128)(2,1)}), bf16[1280,512]{1,0:T(8,128)(2,1)}) %all-gather.9.cloned.1.call-update) | async-done | bytes 1310736 | tf_op jit(solution)/shard_map/all_gather | solution.py:133
  394.1 5.5 fusion.83
  405.6 27.1 %collective-permute-done.6 = bf16[320,1024]{1,0:T(8,128)(2,1)S(1)} collective-permute-done((bf16[320,1024]{1,0:T(8,128)(2,1)S(1)}, bf16[320,1024]{1,0:T(8,128)(2,1)S(1)}, u32[]{:S(2)}, u32[]{:S(2)}) %collective-permute-start.6) | collective-permute-done | bytes 655392 | tf_op jit(solution)/shard_map/ppermute | solution.py:32
  432.8 20.6 %collective-permute-start.8 = (bf16[320,1024]{1,0:T(8,128)(2,1)S(1)}, bf16[320,1024]{1,0:T(8,128)(2,1)S(1)}, u32[]{:S(2)}, u32[]{:S(2)}) collective-permute-start(bf16[320,1024]{1,0:T(8,128)(2,1)S(1)} %collective-permute-done.6), channel_id=1, source_target_pairs={{0,1},{1,2},{2,3},{3,0},{4,5},{5,6},{6,7},{7,4},{8,9},{9,10},{10,1... | collective-permute-start | bytes 1966088 | tf_op jit(solution)/shard_map/ppermute | solution.py:32
  453.4 11.2 collective-permute-done.7
  464.7 23.1 %collective-permute-done.8 = bf16[320,1024]{1,0:T(8,128)(2,1)S(1)} collective-permute-done((bf16[320,1024]{1,0:T(8,128)(2,1)S(1)}, bf16[320,1024]{1,0:T(8,128)(2,1)S(1)}, u32[]{:S(2)}, u32[]{:S(2)}) %collective-permute-start.8) | collective-permute-done | bytes 655392 | tf_op jit(solution)/shard_map/ppermute | solution.py:32
  489.4 6.0 fusion.87
  496.8 36.6 %reduce-scatter.21.cloned.1.call-done = f32[320,1024]{1,0:T(8,128)} async-done(((f32[1280,1024]{1,0:T(8,128)}), f32[320,1024]{1,0:T(8,128)}) %reduce-scatter.21.cloned.1.call-update) | async-done | bytes 1310736 | tf_op jit(solution)/shard_map/reduce_scatter | solution.py:139
  536.5 5.0 psum.172
  547.1 15.6 collective-permute-done.3
  562.8 11.9 collective-permute-done.4
  574.8 14.2 collective-permute-done.5
  590.6 6.4 fusion.84
  597.0 9.5 fusion.85
  606.6 15.1 reduce-scatter.29.cloned.1.call-done
  621.7 89.5 %reduce-scatter.23.cloned.1.call-done = f32[1280,704]{0,1:T(8,128)} async-done(((f32[1280,1408]{0,1:T(8,128)}), f32[1280,704]{0,1:T(8,128)}) %reduce-scatter.23.cloned.1.call-update) | async-done | bytes 3604496 | tf_op jit(solution)/shard_map/reduce_scatter | solution.py:127
  711.2 89.4 %reduce-scatter.25.cloned.1.call-done = f32[1280,704]{0,1:T(8,128)} async-done(((f32[1280,1408]{0,1:T(8,128)}), f32[1280,704]{0,1:T(8,128)}) %reduce-scatter.25.cloned.1.call-update) | async-done | bytes 3604496 | tf_op jit(solution)/shard_map/reduce_scatter | solution.py:127
  800.5 6.6 multiply_convert_fusion
  808.7 48.7 %all-gather.13.cloned.1.call-done = bf16[1280,1408]{0,1:T(8,128)(2,1)} async-done(((bf16[1280,704]{0,1:T(8,128)(2,1)}), bf16[1280,1408]{0,1:T(8,128)(2,1)}) %all-gather.13.cloned.1.call-update) | async-done | bytes 3604496 | tf_op jit(solution)/shard_map/all_gather | solution.py:133
  857.5 8.0 fusion.88
  865.5 44.3 %all-gather.15.cloned.1.call-done = bf16[1280,1408]{0,1:T(8,128)(2,1)} async-done(((bf16[1280,704]{0,1:T(8,128)(2,1)}), bf16[1280,1408]{0,1:T(8,128)(2,1)}) %all-gather.15.cloned.1.call-update) | async-done | bytes 3604496 | tf_op jit(solution)/shard_map/all_gather | solution.py:133
  909.8 11.2 convolution_add_fusion
  921.0 40.9 %all-gather.11.cloned.1.call-done = bf16[1280,1408]{0,1:T(8,128)(2,1)} async-done(((bf16[1280,704]{0,1:T(8,128)(2,1)}), bf16[1280,1408]{0,1:T(8,128)(2,1)}) %all-gather.11.cloned.1.call-update) | async-done | bytes 3604496 | tf_op jit(solution)/shard_map/all_gather | solution.py:133
  962.0 8.0 fusion.86
  970.1 88.7 %reduce-scatter.31.cloned.1.call-done = f32[320,1024]{1,0:T(8,128)} async-done(((f32[1280,1024]{1,0:T(8,128)}), f32[320,1024]{1,0:T(8,128)}) %reduce-scatter.31.cloned.1.call-update) | async-done | bytes 1310736 | tf_op jit(solution)/shard_map/reduce_scatter | solution.py:139
  1058.8 97.1 %reduce-scatter.27.cloned.1.call-done = f32[320,1024]{1,0:T(8,128)} async-done(((f32[1280,1024]{1,0:T(8,128)}), f32[320,1024]{1,0:T(8,128)}) %reduce-scatter.27.cloned.1.call-update) | async-done | bytes 1310736 | tf_op jit(solution)/shard_map/reduce_scatter | solution.py:139
  1171.2 15.7 collective-permute-done.9
  1186.9 10.4 collective-permute-start.11
  1200.3 12.4 collective-permute-done.11
  1219.1 7.8 convolution_convert_fusion.1
  1226.9 5.7 convolution_convert_fusion.2
  1232.6 21.2 %reduce-scatter.33.cloned.1.call-done = f32[1280,256]{1,0:T(8,128)} async-done(((f32[1280,512]{1,0:T(8,128)}), f32[1280,256]{1,0:T(8,128)}) %reduce-scatter.33.cloned.1.call-update) | async-done | bytes 1310736 | tf_op jit(solution)/shard_map/reduce_scatter | solution.py:127
  1257.5 5.0 psum.174
  1265.2 8.5 convolution_convert_fusion
  1276.7 12.8 all-gather.17.cloned.1.call-done
  1289.5 9.7 convolution_bitcast_fusion
  1299.2 10.7 fusion.5
  1312.7 5.3 broadcast.114
  1318.0 136.4 %while.35 = (s32[]{:T(128)}, f32[1,256,512]{2,1,0:T(8,128)S(1)}, f32[20,1,256,512]{3,2,1,0:T(8,128)}, f32[20,1,256]{2,1,0:T(1,128)S(1)}, f32[20,1,256,512]{2,3,0...) while((s32[]{:T(128)}, f32[1,256,512]{2,1,0:T(8,128)S(1)}, ...), condition=%wide.region_28.29_spmd.clone, body=%wide.region_26.28_spmd.clone.sunk | while | flops 786180 | bytes 5249168 | solution.py:96
  1454.5 10.9 fusion.50
  1465.5 9.8 fusion.13
  1482.9 78.4 %all-reduce.11 = bf16[1280,512]{1,0:T(8,128)(2,1)S(1)} all-reduce(f32[1280,512]{1,0:T(8,128)} %bitcast.223), channel_id=1, replica_groups=mesh['dp'=4,'row'=2,'col'=4] {'row'}, use_global_device_ids=true, to_apply=%region_29.30 | all-reduce | flops 655360 | bytes 3932160 | tf_op jit(solution)/shard_map/psum | solution.py:276
  1574.9 11.5 all-gather.19.cloned.1.call-done
  1608.7 23.4 %all-reduce.3 = (bf16[16,512]{1,0:T(8,128)(2,1)S(1)}, bf16[512]{0:T(512)(128)(2,1)S(1)}) all-reduce(bf16[16,512]{1,0:T(8,128)(2,1)S(1)} %convolution_dynamic-update-slice_fusion, bf16[512]{0:T(512)(128)(2,1)S(1)} %dynamic_update_slice.98), channel_id=1, replica_groups=mesh['dp'=4,'row'=2,'col'=4] {'dp','row'}, use_global_device_ids=true, to_apply=%region_43.44 | all-reduce | flops 8704 | bytes 34816 | tf_op jit(solution)/shard_map/psum | solution.py:338
  1634.0 38.8 %psum.176 = bf16[1280,16]{0,1:T(8,128)(2,1)S(1)} all-reduce(f32[1280,16]{0,1:T(8,128)S(1)} %fusion.60), channel_id=1, replica_groups=mesh['dp'=4,'row'=2,'col'=4] {'row','col'}, use_global_device_ids=true, to_apply=%region_33.34 | all-reduce | flops 20480 | bytes 122880 | tf_op jit(solution)/shard_map/psum | solution.py:303
  1675.0 12.6 psum.183
  1688.3 148.1 %all-reduce.9.cloned.1.call-done = (bf16[1024,512]{1,0:T(8,128)(2,1)}, bf16[1024,512]{1,0:T(8,128)(2,1)}, bf16[1024,512]{1,0:T(8,128)(2,1)}, bf16[1024,512]{1,0:...) async-done(((bf16[1024,512]{1,0:T(8,128)(2,1)}, bf16[1024,512]{1,0:T(8,128)(2,1)}, ...) | async-done | bytes 13893648 | tf_op jit(solution)/shard_map/psum | solution.py:326
  1855.7 76.9 %reduce-scatter.35.cloned.1.call-done = f32[320,1024]{1,0:T(8,128)} async-done(((f32[1280,1024]{1,0:T(8,128)}), f32[320,1024]{1,0:T(8,128)}) %reduce-scatter.35.cloned.1.call-update) | async-done | bytes 1310736 | tf_op jit(solution)/shard_map/reduce_scatter | solution.py:139
  1940.6 33.8 %all-reduce.1 = (f32[1024]{0:T(1024)}, f32[256]{0:T(256)}, f32[1024]{0:T(1024)}) all-reduce(f32[1024]{0:T(1024)S(1)} %get-tuple-element.257, f32[256]{0:T(256)S(1)} %copy-done.73, f32[1024]{0:T(1024)S(1)} %copy-done.68), channel_id=1, replica_groups=mesh['dp'=4,'row'=2,'col'=4] {'dp','col'}, use_global_device_ids=true, to_apply=%region_37.38 | all-reduce | flops 2304 | bytes 18432 | tf_op jit(solution)/shard_map/psum | solution.py:336
  (522 shorter events, 369.9 us)
Async XLA Ops:
  7.2 583.4 %copy-start = (bf16[1024,1408]{1,0:T(8,128)(2,1)S(1)}, bf16[1024,1408]{1,0:T(8,128)(2,1)}, u32[]{:S(2)}) copy-start(bf16[1024,1408]{1,0:T(8,128)(2,1)} %param.34) | copy-start | bytes 8650756
  7.2 192.2 %reduce-scatter.13.cloned.1.call-start = ((), (), s32[]{:S(2)}) async-start(), calls=%async_computation.12 | async-start | bytes 3932160 | tf_op jit(solution)/shard_map/reduce_scatter | solution.py:127
  18.2 19.9 %collective-permute-start = (bf16[320,1024]{1,0:T(8,128)(2,1)S(1)}, bf16[320,1024]{1,0:T(8,128)(2,1)}, u32[]{:S(2)}, u32[]{:S(2)}) collective-permute-start(bf16[320,1024]{1,0:T(8,128)(2,1)S(1)} %get-tuple-element.314), channel_id=1, source_target_pairs={{0,1},{1,2},{2,3},{3,0},{4,5},{5,6},{6,7},{7,4},{8,9},{9,10},{10,1... | collective-permute-start | bytes 1966088 | tf_op jit(solution)/shard_map/ppermute | solution.py:32
  20.3 30.7 %collective-permute-start.1 = (bf16[320,1024]{1,0:T(8,128)(2,1)S(1)}, bf16[320,1024]{1,0:T(8,128)(2,1)}, u32[]{:S(2)}, u32[]{:S(2)}) collective-permute-start(bf16[320,1024]{1,0:T(8,128)(2,1)S(1)} %get-tuple-element.314), channel_id=1, source_target_pairs={{0,3},{1,0},{2,1},{3,2},{4,7},{5,4},{6,5},{7,6},{8,11},{9,8},{10,9... | collective-permute-start | bytes 1966088 | tf_op jit(solution)/shard_map/ppermute | solution.py:37
  38.1 26.0 %collective-permute-start.2 = (bf16[320,1024]{1,0:T(8,128)(2,1)}, bf16[320,1024]{1,0:T(8,128)(2,1)}, u32[]{:S(2)}, u32[]{:S(2)}) collective-permute-start(bf16[320,1024]{1,0:T(8,128)(2,1)} %collective-permute-done), channel_id=1, source_target_pairs={{0,1},{1,2},{2,3},{3,0},{4,5},{5,6},{6,7},{7,4},{8,9},{9,10},{10,1... | collective-permute-start | bytes 1966088 | tf_op jit(solution)/shard_map/ppermute | solution.py:32
  49.5 16.6 copy-start.82
  70.9 133.1 %reduce-scatter.15.cloned.1.call-start = ((), (), s32[]{:S(2)}) async-start(), calls=%async_computation.13 | async-start | bytes 3932160 | tf_op jit(solution)/shard_map/reduce_scatter | solution.py:127
  76.0 250.4 %reduce-scatter.17.cloned.1.call-start = ((), (), s32[]{:S(2)}) async-start(), calls=%async_computation.14 | async-start | bytes 3932160 | tf_op jit(solution)/shard_map/reduce_scatter | solution.py:127
  76.7 193.5 %copy-start.53 = (f32[64,64]{1,0:T(8,128)}, f32[64,64]{1,0:T(8,128)S(1)}, u32[]{:S(2)}) copy-start(f32[64,64]{1,0:T(8,128)S(1)} %fusion.52) | copy-start | bytes 49156
  84.5 110.2 %copy-start.71 = (bf16[16,512]{1,0:T(8,128)(2,1)S(1)}, bf16[16,512]{1,0:T(8,128)(2,1)}, u32[]{:S(2)}) copy-start(bf16[16,512]{1,0:T(8,128)(2,1)} %param.29) | copy-start | bytes 49156
  287.5 79.3 %reduce-scatter.19.cloned.1.call-start = ((), (), s32[]{:S(2)}) async-start(), calls=%async_computation.15 | async-start | bytes 3932160 | tf_op jit(solution)/shard_map/reduce_scatter | solution.py:127
  293.0 101.1 %all-gather.9.cloned.1.call-start = ((), (), s32[]{:S(2)}) async-start(), calls=%async_computation.16 | async-start | bytes 1966080 | tf_op jit(solution)/shard_map/all_gather | solution.py:133
  293.7 76.1 %copy-start.69 = (f32[256]{0:T(256)}, f32[256]{0:T(256)S(1)}, u32[]{:S(2)}) copy-start(f32[256]{0:T(256)S(1)} %convert_element_type.167) | copy-start | bytes 3076
  369.8 163.6 %reduce-scatter.21.cloned.1.call-start = ((), (), s32[]{:S(2)}) async-start(), calls=%async_computation.17 | async-start | bytes 6553600 | tf_op jit(solution)/shard_map/reduce_scatter | solution.py:139
  399.7 222.0 %reduce-scatter.29.cloned.1.call-start = ((), (), s32[]{:S(2)}) async-start(), calls=%async_computation.22 | async-start | bytes 10813440 | tf_op jit(solution)/shard_map/reduce_scatter | solution.py:127
  401.8 31.0 %collective-permute-start.6 = (bf16[320,1024]{1,0:T(8,128)(2,1)S(1)}, bf16[320,1024]{1,0:T(8,128)(2,1)S(1)}, u32[]{:S(2)}, u32[]{:S(2)}) collective-permute-start(bf16[320,1024]{1,0:T(8,128)(2,1)S(1)} %get-tuple-element.306), channel_id=1, source_target_pairs={{0,1},{1,2},{2,3},{3,0},{4,5},{5,6},{6,7},{7,4},{8,9},{9,10},{10,1... | collective-permute-start | bytes 1966088 | tf_op jit(solution)/shard_map/ppermute | solution.py:32
  403.3 61.4 %collective-permute-start.7 = (bf16[320,1024]{1,0:T(8,128)(2,1)S(1)}, bf16[320,1024]{1,0:T(8,128)(2,1)S(1)}, u32[]{:S(2)}, u32[]{:S(2)}) collective-permute-start(bf16[320,1024]{1,0:T(8,128)(2,1)S(1)} %get-tuple-element.306), channel_id=1, source_target_pairs={{0,3},{1,0},{2,1},{3,2},{4,7},{5,4},{6,5},{7,6},{8,11},{9,8},{10,9... | collective-permute-start | bytes 1966088 | tf_op jit(solution)/shard_map/ppermute | solution.py:37
  432.8 55.0 %collective-permute-start.8 = (bf16[320,1024]{1,0:T(8,128)(2,1)S(1)}, bf16[320,1024]{1,0:T(8,128)(2,1)S(1)}, u32[]{:S(2)}, u32[]{:S(2)}) collective-permute-start(bf16[320,1024]{1,0:T(8,128)(2,1)S(1)} %collective-permute-done.6), channel_id=1, source_target_pairs={{0,1},{1,2},{2,3},{3,0},{4,5},{5,6},{6,7},{7,4},{8,9},{9,10},{10,1... | collective-permute-start | bytes 1966088 | tf_op jit(solution)/shard_map/ppermute | solution.py:32
  453.4 36.0 %copy-start.76 = (bf16[1408,1024]{1,0:T(8,128)(2,1)S(1)}, bf16[1408,1024]{1,0:T(8,128)(2,1)}, u32[]{:S(2)}) copy-start(bf16[1408,1024]{1,0:T(8,128)(2,1)} %param.36) | copy-start | bytes 8650756
  495.4 38.0 %copy-start.20 = (bf16[320,1024]{1,0:T(8,128)(2,1)S(1)}, bf16[320,1024]{1,0:T(8,128)(2,1)}, u32[]{:S(2)}) copy-start(bf16[320,1024]{1,0:T(8,128)(2,1)} %param.21) | copy-start | bytes 1966084
  495.4 215.8 %reduce-scatter.23.cloned.1.call-start = ((), (), s32[]{:S(2)}) async-start(), calls=%async_computation.18 | async-start | bytes 10813440 | tf_op jit(solution)/shard_map/reduce_scatter | solution.py:127
  543.3 19.5 collective-permute-start.3
  544.5 30.2 %collective-permute-start.4 = (bf16[320,1024]{1,0:T(8,128)(2,1)S(1)}, bf16[320,1024]{1,0:T(8,128)(2,1)S(1)}, u32[]{:S(2)}, u32[]{:S(2)}) collective-permute-start(bf16[320,1024]{1,0:T(8,128)(2,1)S(1)} %get-tuple-element.308), channel_id=1, source_target_pairs={{0,3},{1,0},{2,1},{3,2},{4,7},{5,4},{6,5},{7,6},{8,11},{9,8},{10,9... | collective-permute-start | bytes 1966088 | tf_op jit(solution)/shard_map/ppermute | solution.py:37
  562.8 26.3 %collective-permute-start.5 = (bf16[320,1024]{1,0:T(8,128)(2,1)S(1)}, bf16[320,1024]{1,0:T(8,128)(2,1)S(1)}, u32[]{:S(2)}, u32[]{:S(2)}) collective-permute-start(bf16[320,1024]{1,0:T(8,128)(2,1)S(1)} %collective-permute-done.3), channel_id=1, source_target_pairs={{0,1},{1,2},{2,3},{3,0},{4,5},{5,6},{6,7},{7,4},{8,9},{9,10},{10,1... | collective-permute-start | bytes 1966088 | tf_op jit(solution)/shard_map/ppermute | solution.py:32
  597.0 203.5 %reduce-scatter.25.cloned.1.call-start = ((), (), s32[]{:S(2)}) async-start(), calls=%async_computation.19 | async-start | bytes 10813440 | tf_op jit(solution)/shard_map/reduce_scatter | solution.py:127
  606.5 250.9 %all-gather.13.cloned.1.call-start = ((), (), s32[]{:S(2)}) async-start(), calls=%async_computation.23 | async-start | bytes 5406720 | tf_op jit(solution)/shard_map/all_gather | solution.py:133
  807.2 102.6 %all-gather.15.cloned.1.call-start = ((), (), s32[]{:S(2)}) async-start(), calls=%async_computation.24 | async-start | bytes 5406720 | tf_op jit(solution)/shard_map/all_gather | solution.py:133
  807.9 154.1 %all-gather.11.cloned.1.call-start = ((), (), s32[]{:S(2)}) async-start(), calls=%async_computation.20 | async-start | bytes 5406720 | tf_op jit(solution)/shard_map/all_gather | solution.py:133
  808.5 250.3 %reduce-scatter.31.cloned.1.call-start = ((), (), s32[]{:S(2)}) async-start(), calls=%async_computation.25 | async-start | bytes 6553600 | tf_op jit(solution)/shard_map/reduce_scatter | solution.py:139
  921.0 41.0 %copy-start.77 = (bf16[1408,1024]{1,0:T(8,128)(2,1)S(1)}, bf16[1408,1024]{1,0:T(8,128)(2,1)}, u32[]{:S(2)}) copy-start(bf16[1408,1024]{1,0:T(8,128)(2,1)} %param.36) | copy-start | bytes 8650756
  921.0 234.9 %reduce-scatter.27.cloned.1.call-start = ((), (), s32[]{:S(2)}) async-start(), calls=%async_computation.21 | async-start | bytes 6553600 | tf_op jit(solution)/shard_map/reduce_scatter | solution.py:139
  970.0 185.9 %copy-start.18 = (f32[320,1024]{1,0:T(8,128)S(1)}, f32[320,1024]{1,0:T(8,128)}, u32[]{:S(2)}) copy-start(f32[320,1024]{1,0:T(8,128)} %get-tuple-element.310) | copy-start | bytes 3932164
  970.0 185.9 %copy-start.63 = (f32[320]{0:T(512)S(1)}, f32[320]{0:T(512)}, u32[]{:S(2)}) copy-start(f32[320]{0:T(512)} %copy-done.62) | copy-start | bytes 3844
  970.0 283.8 %reduce-scatter.33.cloned.1.call-start = ((), (), s32[]{:S(2)}) async-start(), calls=%async_computation.26 | async-start | bytes 3932160 | tf_op jit(solution)/shard_map/reduce_scatter | solution.py:127
  1167.4 19.5 collective-permute-start.9
  1168.9 31.3 %collective-permute-start.10 = (bf16[320,1024]{1,0:T(8,128)(2,1)S(1)}, bf16[320,1024]{1,0:T(8,128)(2,1)S(1)}, u32[]{:S(2)}, u32[]{:S(2)}) collective-permute-start(bf16[320,1024]{1,0:T(8,128)(2,1)S(1)} %get-tuple-element.303), channel_id=1, source_target_pairs={{0,3},{1,0},{2,1},{3,2},{4,7},{5,4},{6,5},{7,6},{8,11},{9,8},{10,9... | collective-permute-start | bytes 1966088 | tf_op jit(solution)/shard_map/ppermute | solution.py:37
  1186.9 25.8 %collective-permute-start.11 = (bf16[320,1024]{1,0:T(8,128)(2,1)S(1)}, bf16[320,1024]{1,0:T(8,128)(2,1)S(1)}, u32[]{:S(2)}, u32[]{:S(2)}) collective-permute-start(bf16[320,1024]{1,0:T(8,128)(2,1)S(1)} %collective-permute-done.9), channel_id=1, source_target_pairs={{0,1},{1,2},{2,3},{3,0},{4,5},{5,6},{6,7},{7,4},{8,9},{9,10},{10,1... | collective-permute-start | bytes 1966088 | tf_op jit(solution)/shard_map/ppermute | solution.py:32
  1197.3 16.9 copy-start.80
  1217.4 72.1 %all-gather.17.cloned.1.call-start = ((), (), s32[]{:S(2)}) async-start(), calls=%async_computation.27 | async-start | bytes 1966080 | tf_op jit(solution)/shard_map/all_gather | solution.py:133
  1226.9 26.9 %copy-start.16 = (f32[1280,256]{1,0:T(8,128)S(1)}, f32[1280,256]{1,0:T(8,128)}, u32[]{:S(2)}) copy-start(f32[1280,256]{1,0:T(8,128)} %reduce-scatter.17.cloned.1.call-done) | copy-start | bytes 3932164
  1226.9 26.9 %copy-start.24 = (f32[1280,256]{1,0:T(8,128)S(1)}, f32[1280,256]{1,0:T(8,128)}, u32[]{:S(2)}) copy-start(f32[1280,256]{1,0:T(8,128)} %reduce-scatter.19.cloned.1.call-done) | copy-start | bytes 3932164
  1226.9 26.9 %copy-start.70 = (f32[256]{0:T(256)S(1)}, f32[256]{0:T(256)}, u32[]{:S(2)}) copy-start(f32[256]{0:T(256)} %copy-done.69) | copy-start | bytes 3076
  1265.1 300.5 %all-gather.23.cloned.1.call-start = ((), (), s32[]{:S(2)}) async-start(), calls=%async_computation.30 | async-start | bytes 1966080 | tf_op jit(solution)/shard_map/all_gather | solution.py:133
  1273.6 15.8 copy-start.9
  1276.2 294.0 %all-gather.21.cloned.1.call-start = ((), (), s32[]{:S(2)}) async-start(), calls=%async_computation.29 | async-start | bytes 1966080 | tf_op jit(solution)/shard_map/all_gather | solution.py:133
  1299.2 10.7 copy-start.29
  1318.0 136.5 %copy-start.4 = (f32[1280,256]{1,0:T(8,128)S(1)}, f32[1280,256]{1,0:T(8,128)}, u32[]{:S(2)}) copy-start(f32[1280,256]{1,0:T(8,128)} %copy-done.3) | copy-start | bytes 3932164
  1318.0 136.5 %copy-start.7 = (f32[1,20,64,256]{3,2,1,0:T(8,128)S(1)}, f32[1,20,64,256]{3,2,1,0:T(8,128)}, u32[]{:S(2)}) copy-start(f32[1,20,64,256]{3,2,1,0:T(8,128)} %copy-done.5) | copy-start | bytes 3932164
  1318.0 136.5 %copy-start.52 = (f32[1,20,1,256]{3,1,2,0:T(8,128)S(1)}, f32[1,20,1,256]{3,1,2,0:T(8,128)}, u32[]{:S(2)}) copy-start(f32[1,20,1,256]{3,1,2,0:T(8,128)} %copy-done.51) | copy-start | bytes 61444
  1454.5 11.0 copy-start.2
  1465.5 9.9 copy-start.13
  1465.5 9.9 copy-start.15
  1465.5 9.9 copy-start.54
  1482.8 103.6 %all-gather.19.cloned.1.call-start = ((), (), s32[]{:S(2)}) async-start(), calls=%async_computation.28 | async-start | bytes 1966080 | tf_op jit(solution)/shard_map/all_gather | solution.py:133
  1561.3 275.1 %all-reduce.9.cloned.1.call-start = ((), (), s32[]{:S(2)}) async-start(), calls=%async_computation.32 | async-start | bytes 27787264 | tf_op jit(solution)/shard_map/psum | solution.py:326
  1591.1 341.6 %reduce-scatter.35.cloned.1.call-start = ((), (), s32[]{:S(2)}) async-start(), calls=%async_computation.31 | async-start | bytes 6553600 | tf_op jit(solution)/shard_map/reduce_scatter | solution.py:139
  1607.8 25.5 %copy-start.72 = (bf16[16,512]{1,0:T(8,128)(2,1)S(1)}, bf16[16,512]{1,0:T(8,128)(2,1)}, u32[]{:S(2)}) copy-start(bf16[16,512]{1,0:T(8,128)(2,1)} %param.29) | copy-start | bytes 49156
  1854.1 78.5 %copy-start.21 = (bf16[320,1024]{1,0:T(8,128)(2,1)S(1)}, bf16[320,1024]{1,0:T(8,128)(2,1)}, u32[]{:S(2)}) copy-start(bf16[320,1024]{1,0:T(8,128)(2,1)} %param.21) | copy-start | bytes 1966084
  1854.1 78.5 %copy-start.57 = (bf16[1024,16]{0,1:T(8,128)(2,1)S(1)}, bf16[1024,16]{0,1:T(8,128)(2,1)}, u32[]{:S(2)}) copy-start(bf16[1024,16]{0,1:T(8,128)(2,1)} %param.28) | copy-start | bytes 98308
  1854.1 78.5 %copy-start.59 = (f32[1024]{0:T(1024)S(1)}, f32[1024]{0:T(1024)}, u32[]{:S(2)}) copy-start(f32[1024]{0:T(1024)} %copy-done.58) | copy-start | bytes 12292
  1854.1 78.5 %copy-start.65 = (f32[320]{0:T(512)S(1)}, f32[320]{0:T(512)}, u32[]{:S(2)}) copy-start(f32[320]{0:T(512)} %copy-done.64) | copy-start | bytes 3844
  1855.7 84.9 %copy-start.67 = (f32[320]{0:T(512)S(1)}, f32[320]{0:T(512)}, u32[]{:S(2)}) copy-start(f32[320]{0:T(512)} %copy-done.66) | copy-start | bytes 3844
  1855.7 84.9 %copy-start.68 = (f32[1024]{0:T(1024)S(1)}, f32[1024]{0:T(1024)}, u32[]{:S(2)}) copy-start(f32[1024]{0:T(1024)} %get-tuple-element.255) | copy-start | bytes 12292
  1855.7 84.9 %copy-start.73 = (f32[256]{0:T(256)S(1)}, f32[256]{0:T(256)}, u32[]{:S(2)}) copy-start(f32[256]{0:T(256)} %get-tuple-element.253) | copy-start | bytes 3076
  (54 other events, 142.6 us)
Sparse Core Ops, SparseCore 0:
  71.0 55.0 reduce-scatter.12
  129.0 64.9 reduce-scatter.14
  287.6 38.7 reduce-scatter.16
  329.1 37.5 reduce-scatter.18
  369.9 24.2 all-gather.8
  399.8 133.5 reduce-scatter.20
  535.7 85.9 reduce-scatter.28
  624.1 87.0 reduce-scatter.22
  713.5 86.9 reduce-scatter.24
  807.3 50.1 all-gather.12
  859.7 50.0 all-gather.14
  911.8 50.0 all-gather.10
  965.0 93.7 reduce-scatter.30
  1061.6 94.2 reduce-scatter.26
  1217.5 36.2 reduce-scatter.32
  1265.2 24.2 all-gather.16
  1290.9 24.2 all-gather.22
  1482.9 38.3 all-gather.20
  1561.4 24.9 all-gather.18
  1591.2 245.1 all-reduce.8
  1838.7 93.9 reduce-scatter.34
